TPU v7x, 32 devices: a whole 2x2x4 slice. The times are simulated.
32 devices in a mesh: row: 4 (over z), col: 8 (over y, x, core).
Axes of the slice: x: 2, y: 2, z: 4, core: 2. Of those that a mesh axis runs over, the one named last changes fastest.
Arguments:
- a_blocks: bfloat16 [4, 8, 108, 138, 138], P('row', 'col'), may hold values from -0.0625 to 0.0625
- a_coord: int32 [4, 8, 108], replicated, may hold values from 0 to 1151, as said below
- b_blocks: bfloat16 [4, 2, 8, 27, 138, 138], P('row', None, 'col'), may hold values from -6 to 6
- b_coord: int32 [4, 2, 8, 27], replicated, may hold values from 0 to 287, as said below
- keep_list: int32 [4, 8, 32], replicated, may hold values from 0 to 63, as said below
- permutation: int32 [64], replicated, may hold values from 0 to 63, as said below
Outputs:
- next_rows: bfloat16 [4, 8, 16, 4, 138, 138], P('row', 'col')
Inputs may be any that keep to these rules, and one draw needn't show every extreme that they name: `a_coord`: codes block (i, k) as i * 72 + k; the entries of one device are distinct; over all devices and both A and B the block columns k take only 18 values, among them 0 and 71. `b_coord`: codes block (k, j) as k * 4 + j; the entries of one device and panel are distinct; k takes the same 18 values as in a_coord. `keep_list`: codes product block (i, j) as i * 4 + j; the entries of one device are distinct. A permutation; the 16 block rows of one device row go to 4 device rows, exactly 4 to each.
All inputs are finite; a program needn't handle non-finite values.
Results may differ from a plain program's by a relative error of at most 0.001.
Values may be sent and summed in bfloat16 or wider, within the bound.
A program may use at most 256 MiB of HBM per device.

v0:
```python
import jax
import jax.numpy as jnp
from jax import lax
from jax.sharding import PartitionSpec as P

KL = 72
BRL = 16
BCL = 4


def shifted(value, axis, steps):
    count = lax.axis_size(axis)
    pairs = [(source, (source + steps) % count) for source in range(count)]
    return lax.ppermute(value, axis, pairs)


def panel_product(a_part, a_codes, b_part, b_codes):
    block_rows = a_codes // KL
    block_cols = a_codes % KL
    wanted = block_cols[:, None] * BCL + jnp.arange(BCL, dtype=jnp.int32)[None, :]
    selector = (b_codes[None, None, :] == wanted[:, :, None]).astype(jnp.bfloat16)
    b_rows = jnp.einsum(
        "sjt,tbc->sjbc", selector, b_part, preferred_element_type=jnp.float32
    ).astype(jnp.bfloat16)
    terms = jnp.einsum("sab,sjbc->sjac", a_part, b_rows, preferred_element_type=jnp.float32)
    placing = (block_rows[:, None] == jnp.arange(BRL, dtype=jnp.int32)[None, :]).astype(jnp.float32)
    return jnp.einsum("si,sjac->ijac", placing, terms, precision=lax.Precision.HIGHEST)


def body(a_blocks, a_coord, b_blocks, b_coord, keep_list, permutation):
    row_count = lax.axis_size("row")
    col_count = lax.axis_size("col")
    slot_count = max(2, BRL // row_count)
    row_here = lax.axis_index("row")
    col_here = lax.axis_index("col")
    row_next = (row_here + 1) % row_count
    col_next = (col_here + 1) % col_count
    a_here = a_blocks[0, 0]
    b_first = b_blocks[0, 0, 0]
    b_second = b_blocks[0, 1, 0]
    at_start = row_here == 0
    own_keep = keep_list[row_here, col_here]
    own_term = panel_product(
        a_here, a_coord[row_here, col_here], b_first, b_coord[row_here, 0, col_here]
    )
    b_sent = jnp.where(at_start, b_second, b_first)
    image_pick = (row_next == 0).astype(jnp.int32)
    block_edge = a_here.shape[-1]
    a_moved = shifted(a_here, "col", -1)
    b_moved = shifted(b_sent, "row", -1)
    later_term = panel_product(
        a_moved, a_coord[row_here, col_next], b_moved, b_coord[row_next, image_pick, col_here]
    )
    all_codes = jnp.arange(BRL * BCL, dtype=jnp.int32)
    keep_mask = jnp.any(all_codes[:, None] == own_keep[None, :], axis=1).reshape(BRL, BCL)
    filtered = jnp.where(
        keep_mask[:, :, None, None], own_term + later_term, jnp.float32(0.0)
    ).astype(jnp.bfloat16)
    targets = permutation.reshape(row_count, BRL)
    owners = targets // BRL
    positions = jnp.arange(BRL, dtype=jnp.int32)
    before = (owners[:, None, :] == owners[:, :, None]) & (
        positions[None, None, :] < positions[None, :, None]
    )
    slot_rank = jnp.sum(before.astype(jnp.int32), axis=2)
    outgoing = jnp.zeros((row_count, slot_count, BCL, block_edge, block_edge), jnp.bfloat16)
    outgoing = outgoing.at[owners[row_here], slot_rank[row_here]].set(filtered, unique_indices=True)
    incoming = lax.all_to_all(outgoing, "row", split_axis=0, concat_axis=0, tiled=True)
    inverse = (
        jnp.zeros_like(permutation)
        .at[permutation]
        .set(jnp.arange(permutation.shape[0], dtype=jnp.int32))
    )
    sources = lax.dynamic_slice_in_dim(inverse, row_here * BRL, BRL)
    flat_slot = sources // BRL * slot_count + slot_rank.reshape(-1)[sources]
    arrived = incoming.reshape(row_count * slot_count, BCL, block_edge, block_edge)[flat_slot]
    return arrived[None, None]


def solution(mesh):
    in_specs = (
        P("row", "col", None, None, None),
        P(),
        P("row", None, "col", None, None, None),
        P(),
        P(),
        P(),
    )
    out_specs = P("row", "col", None, None, None, None)
    return jax.shard_map(body, mesh=mesh, in_specs=in_specs, out_specs=out_specs, check_vma=False)
```

profile of v0, /device:TPU:0, one launch (start us, length us, event | category | flops | bytes accessed | tf_op | source)
XLA Modules:
  0.0 599.8 jit_solution(10886706027828944185)
XLA Ops:
  0.0 0.0 copy-start
  0.0 13.2 %fusion.35 = (bf16[1,1,1,27,138,138]{5,1,4,3,2,0:T(2,128)(2,1)}, bf16[1,1,1,27,138,138]{5,1,4,3,2,0:T(2,128)(2,1)}) fusion(bf16[1,2,1,27,138,138]{5,1,4,3,2,0:T(2,128)(2,1)} %param.8), kind=kLoop, calls=%fused_computation.80 | loop fusion | bytes 4113504 | tf_op jit(solution)/shard_map/slice | solution.py:40
  13.2 3.8 bitcast_select_fusion
  16.9 2.4 copy.31
  19.3 5.1 collective-permute-start
  24.4 1.8 collective-permute-start.1
  26.2 1.3 fusion.22
  27.5 0.7 fusion.29
  28.2 11.8 %convolution_convert_fusion.1 = bf16[108,4,138,138]{0,3,2,1:T(8,128)(2,1)} fusion(bf16[1,1,1,27,138,138]{5,1,4,3,2,0:T(2,128)(2,1)} %get-tuple-element.6, s32[108,4]{0,1:T(4,128)S(1)} %iota_add_fusion.1, s32[27]{0:T(128)S(1)} %get-tuple-element.8), kind=kOutput, calls=%fused_computation.7 | convolution fusion | flops 452497088 | bytes 17484228 | tf_op jit(solution)/shard_map/sjt,tbc->sjbc/dot_general | solution.py:22
  40.0 56.5 %copy.26 = bf16[108,4,138,138]{2,3,1,0:T(8,128)(2,1)} copy(bf16[108,4,138,138]{0,3,2,1:T(8,128)(2,1)} %convolution_convert_fusion.1) | data formatting | bytes 32908032 | tf_op jit(solution)/shard_map/convert_element_type | solution.py:24
  96.6 13.6 %copy.38 = bf16[108,138,138,1]{2,1,3,0:T(8,128)(2,1)} copy(bf16[108,138,138,1]{0,2,1,3:T(8,128)(2,1)} %bitcast.15) | data formatting | bytes 8227008 | tf_op jit(solution)/shard_map/squeeze | solution.py:38
  110.2 0.0 copy-start.3
  110.2 34.9 %convolution_bitcast_fusion.1 = f32[108,4,138,138]{2,3,1,0:T(8,128)} fusion(bf16[108,4,138,138]{2,3,1,0:T(8,128)(2,1)} %copy.26, bf16[108,138,138,1]{2,1,3,0:T(8,128)(2,1)} %copy.38), kind=kOutput, calls=%fused_computation.5 | convolution fusion | flops 2270654208 | bytes 53475552 | tf_op jit(solution)/shard_map/sab,sjbc->sjac/dot_general | solution.py:25
  145.1 0.0 copy-done.3
  145.1 0.1 reshape.248
  145.2 60.5 %copy.28 = f32[108,4,138,138]{0,3,2,1:T(8,128)} copy(f32[108,4,138,138]{2,3,1,0:T(8,128)} %convolution_bitcast_fusion.1) | data formatting | bytes 65816064 | tf_op jit(solution)/shard_map/sab,sjbc->sjac/transpose | solution.py:25
  205.7 0.0 copy-done
  205.7 0.1 fusion.12
  205.8 0.1 broadcast_in_dim.25
  205.9 0.1 copy.24
  206.0 0.2 convert_reduce_fusion
  206.3 37.7 %fusion.14 = f32[16,4,138,138]{3,0,2,1:T(8,128)} fusion(f32[108,4,138,138]{0,3,2,1:T(8,128)} %copy.28, s32[108]{0:T(128)S(1)} %get-tuple-element.12), kind=kOutput, calls=%fused_computation.29 | convolution fusion | flops 1579587328 | bytes 37783728 | tf_op jit(solution)/shard_map/si,sjac->ijac/dot_general | solution.py:27
  244.0 0.0 collective-permute-done
  244.0 10.0 %convolution_convert_fusion = bf16[108,4,138,138]{0,3,2,1:T(8,128)(2,1)} fusion(bf16[27,138,138]{2,1,0:T(8,128)(2,1)S(1)} %collective-permute-done, s32[108,4]{0,1:T(4,128)S(1)} %iota_add_fusion, s32[27]{0:T(128)S(1)} %get-tuple-element.7), kind=kOutput, calls=%fused_computation.6 | convolution fusion | flops 452497088 | bytes 17484228 | tf_op jit(solution)/shard_map/sjt,tbc->sjbc/dot_general | solution.py:22
  254.0 56.5 %copy.33 = bf16[108,4,138,138]{2,3,1,0:T(8,128)(2,1)} copy(bf16[108,4,138,138]{0,3,2,1:T(8,128)(2,1)} %convolution_convert_fusion) | data formatting | bytes 32908032 | tf_op jit(solution)/shard_map/convert_element_type | solution.py:24
  310.5 0.0 collective-permute-done.1
  310.5 13.6 %copy.41 = bf16[108,138,138,1]{2,1,3,0:T(8,128)(2,1)} copy(bf16[108,138,138,1]{0,2,1,3:T(8,128)(2,1)} %bitcast.27) | data formatting | bytes 8227008 | tf_op jit(solution)/shard_map/ppermute | solution.py:14
  324.1 35.1 %convolution_bitcast_fusion = f32[108,4,138,138]{2,3,1,0:T(8,128)} fusion(bf16[108,4,138,138]{2,3,1,0:T(8,128)(2,1)} %copy.33, bf16[108,138,138,1]{2,1,3,0:T(8,128)(2,1)} %copy.41), kind=kOutput, calls=%fused_computation.4 | convolution fusion | flops 2270654208 | bytes 53475552 | tf_op jit(solution)/shard_map/sab,sjbc->sjac/dot_general | solution.py:25
  359.2 0.0 copy-start.2
  359.2 60.5 %copy.35 = f32[108,4,138,138]{0,3,2,1:T(8,128)} copy(f32[108,4,138,138]{2,3,1,0:T(8,128)} %convolution_bitcast_fusion) | data formatting | bytes 65816064 | tf_op jit(solution)/shard_map/sab,sjbc->sjac/transpose | solution.py:25
  419.7 0.0 copy-done.2
  419.7 37.7 %select_convert_fusion = bf16[16,4,138,138]{3,0,2,1:T(8,128)(2,1)} fusion(f32[16,4,138,138]{3,0,2,1:T(8,128)} %fusion.14, pred[16,4]{0,1:T(4,128)(4,1)S(1)} %copy.24, f32[108,4,138,138]{0,3,2,1:T(8,128)} %copy.35, s32[108]{0:T(128)S(1)} %copy-done.2), kind=kOutput, calls=%fused_computation.8 | convolution fusion | flops 1583243776 | bytes 40221424 | tf_op jit(solution)/shard_map/si,sjac->ijac/dot_general | solution.py:27
  457.5 7.8 %copy.36 = bf16[16,4,138,138]{3,1,2,0:T(4,128)(2,1)} copy(bf16[16,4,138,138]{3,0,2,1:T(8,128)(2,1)} %select_convert_fusion) | data formatting | bytes 4875264 | tf_op jit(solution)/shard_map/convert_element_type | solution.py:58
  465.3 3.3 broadcast_in_dim.24
  468.6 18.4 %scatter_fusion = bf16[4,4,4,138,138]{4,2,3,1,0:T(4,128)(2,1)} fusion(bf16[4,4,4,138,138]{4,2,3,1,0:T(4,128)(2,1)} %broadcast_in_dim.24, s32[16]{0:T(128)S(1)} %fusion.32, bf16[16,4,138,138]{3,1,2,0:T(4,128)(2,1)} %copy.36), kind=kCustom, calls=%fused_computation.2 | custom fusion | bytes 7313024 | tf_op jit(solution)/shard_map/scatter | solution.py:67
  486.9 0.0 copy-start.4
  486.9 5.0 all-to-all-start
  492.0 0.0 copy-start.1
  492.0 0.1 reshape.250
  492.1 0.0 copy-done.4
  492.1 0.8 scatter_custom_fusion.1
  492.8 0.1 compare_select_fusion.4
  492.9 0.7 gather_fusion
  493.6 0.1 compare_select_fusion
  493.7 97.8 %all-to-all-done = bf16[4,4,4,138,138]{4,2,3,1,0:T(4,128)(2,1)} async-done(((bf16[4,4,4,138,138]{4,2,3,1,0:T(4,128)(2,1)}), bf16[4,4,4,138,138]{4,2,3,1,0:T(4,128)(2,1)}, u32[]{:S(2)}, u32[]{:S(2)}) %all-to-all-start) | async-done | bytes 2437664 | tf_op jit(solution)/shard_map/all_to_all | solution.py:68
  591.5 8.1 %gather_fusion.1 = bf16[16,4,138,138]{3,1,2,0:T(4,128)(2,1)} fusion(bf16[16,4,138,138]{3,1,2,0:T(4,128)(2,1)} %bitcast.29, s32[1024]{0:T(1024)S(1)} %pad_clamp_fusion), kind=kCustom, calls=%fused_computation.1 | custom fusion | bytes 4875328 | tf_op jit(solution)/shard_map/gather | solution.py:76
  599.6 0.0 copy-done.1
  (10 shorter events, 0.1 us)
Async XLA Ops:
  0.0 205.7 %copy-start = (s32[4,8,32]{2,1,0:T(8,128)S(1)}, s32[4,8,32]{2,1,0:T(8,128)}, u32[]{:S(2)}) copy-start(s32[4,8,32]{2,1,0:T(8,128)} %param.10) | copy-start | bytes 12292
  19.3 224.6 %collective-permute-start = (bf16[27,138,138]{2,1,0:T(8,128)(2,1)}, bf16[27,138,138]{2,1,0:T(8,128)(2,1)S(1)}, u32[]{:S(2)}, u32[]{:S(2)}) collective-permute-start(bf16[27,138,138]{2,1,0:T(8,128)(2,1)} %copy.31), channel_id=1, source_target_pairs={{0,24},{8,0},{16,8},{24,16},{1,25},{9,1},{17,9},{25,17},{2,26},{10... | collective-permute-start | bytes 3085136 | tf_op jit(solution)/shard_map/ppermute | solution.py:14
  24.4 286.1 %collective-permute-start.1 = (bf16[108,138,138]{0,2,1:T(8,128)(2,1)}, bf16[108,138,138]{0,2,1:T(8,128)(2,1)}, u32[]{:S(2)}, u32[]{:S(2)}) collective-permute-start(bf16[108,138,138]{0,2,1:T(8,128)(2,1)} %bitcast.14), channel_id=1, source_target_pairs={{0,7},{1,0},{2,1},{3,2},{4,3},{5,4},{6,5},{7,6},{8,15},{9,8},{10,9... | collective-permute-start | bytes 12340520 | tf_op jit(solution)/shard_map/ppermute | solution.py:14
  110.2 34.9 %copy-start.3 = (s32[64]{0:T(128)S(1)}, s32[64]{0:T(128)}, u32[]{:S(2)}) copy-start(s32[64]{0:T(128)} %param.11) | copy-start | bytes 772
  359.2 60.5 %copy-start.2 = (s32[108]{0:T(128)S(1)}, s32[108]{0:T(128)}, u32[]{:S(2)}) copy-start(s32[108]{0:T(128)} %get-tuple-element.9) | copy-start | bytes 1300
  486.9 5.1 copy-start.4
  486.9 104.6 %all-to-all-start = ((bf16[4,4,4,138,138]{4,2,3,1,0:T(4,128)(2,1)}), bf16[4,4,4,138,138]{4,2,3,1,0:T(4,128)(2,1)}, u32[]{:S(2)}, u32[]{:S(2)}) async-start(bf16[4,4,4,138,138]{4,2,3,1,0:T(4,128)(2,1)} %scatter_fusion), calls=%async_computation | async-start | bytes 9043968 | tf_op jit(solution)/shard_map/all_to_all | solution.py:68
  492.0 107.6 %copy-start.1 = (s32[4,8,32]{2,1,0:T(8,128)S(1)}, s32[4,8,32]{2,1,0:T(8,128)}, u32[]{:S(2)}) copy-start(s32[4,8,32]{2,1,0:T(8,128)} %param.10) | copy-start | bytes 12292
where the time goes:
time: 610 us; the launch traced here: 600 us
  local copies, waits for them, and re-layouts  317 us (52%)
  matrix products  167 us (27%)
  waiting for transfers between devices  97.8 us (16%)
  starting transfers between devices  11.9 us (2%)
    transpose x2, local copies, waits for them, and re-layouts, panel_product(): jnp.einsum('sab,sjbc->sjac', a_part, b_rows, preferred_element_type=jnp.f...  121 us
    convert_element_type x2, local copies, waits for them, and re-layouts, panel_product(): b_rows = jnp.einsum('sjt,tbc->sjbc', selector, b_part, preferred_element_...  113 us
    all_to_all x1, waiting for transfers between devices, body(): lax.all_to_all(outgoing, 'row', split_axis=0, concat_axis=0, tiled=True)  97.8 us
    dot_general x2, matrix products, panel_product(): jnp.einsum('si,sjac->ijac', placing, terms, precision=lax.Precision.HIGHEST)  75.4 us
    dot_general x2, matrix products, panel_product(): jnp.einsum('sab,sjbc->sjac', a_part, b_rows, preferred_element_type=jnp.f...  70 us
    dot_general x2, matrix products, panel_product(): jnp.einsum('sjt,tbc->sjbc', selector, b_part, preferred_element_type=jnp....  21.8 us
    scatter x1, local copies, waits for them, and re-layouts, body(): outgoing.at[owners[row_here], slot_rank[row_here]]  18.4 us
    ppermute x1, local copies, waits for them, and re-layouts, shifted(): return lax.ppermute(value, axis, pairs)  13.6 us
  transfers between devices with their start and end apart: 3, of which 1 were waited for; matrix products, arithmetic and copies ran while one was open for 48% of the time, Pallas kernels for 0%

commit v1 on v0

v1 whole, which is shorter than its diff:
```python
import jax
import jax.numpy as jnp
from jax import lax
from jax.experimental import pallas as pl
from jax.experimental.pallas import tpu as pltpu
from jax.sharding import PartitionSpec as P

KL = 72
BRL = 16
BCL = 4
LANES = 128
SMEM = pl.BlockSpec(memory_space=pltpu.SMEM)
VMEM = pl.BlockSpec(memory_space=pltpu.VMEM)


def shifted(value, axis, steps):
    count = lax.axis_size(axis)
    pairs = [(source, (source + steps) % count) for source in range(count)]
    return lax.ppermute(value, axis, pairs)


def strip_kernel(home_ref, col_ref, main_ref, rest_ref, out_ref):
    out_ref[...] = jnp.zeros_like(out_ref)
    rest = rest_ref.shape[-1]

    def step(t, carry):
        home, j = home_ref[t], col_ref[t]
        out_ref[home, :, pl.ds(pl.multiple_of(j * LANES, LANES), LANES)] = main_ref[t]
        tail = rest_ref[t]
        for at in range(BCL):

            @pl.when(j == at)
            def _():
                out_ref[home, :, BCL * LANES + at * rest : BCL * LANES + (at + 1) * rest] = tail

        return carry

    lax.fori_loop(0, main_ref.shape[0], step, 0)


def build_strips(main, rest, home, col):
    slots, edge, _ = main.shape
    return pl.pallas_call(
        strip_kernel,
        out_shape=jax.ShapeDtypeStruct((slots + 1, edge, (BCL + 1) * LANES), jnp.bfloat16),
        in_specs=[SMEM, SMEM, VMEM, VMEM],
        out_specs=VMEM,
        name="strips",
    )(home, col, main, rest)


def first_kernel(row_ref, home_ref, a_ref, strip_ref, acc_ref):
    acc_ref[...] = jnp.zeros_like(acc_ref)

    def step(s, carry):
        i = row_ref[s]
        acc_ref[i] += jnp.dot(a_ref[s], strip_ref[home_ref[s]], preferred_element_type=jnp.float32)
        return carry

    lax.fori_loop(0, a_ref.shape[0], step, 0)


def second_kernel(row_ref, home_ref, place_ref, a_ref, strip_ref, start_ref, mask_ref, out_ref, acc_ref):
    acc_ref[...] = start_ref[...]

    def step(s, carry):
        i = row_ref[s]
        acc_ref[i] += jnp.dot(a_ref[s], strip_ref[home_ref[s]], preferred_element_type=jnp.float32)
        return carry

    lax.fori_loop(0, a_ref.shape[0], step, 0)

    def put(i, carry):
        kept = jnp.where(mask_ref[i] > 0.0, acc_ref[i], 0.0)
        out_ref[place_ref[i]] = kept.astype(jnp.bfloat16)
        return carry

    lax.fori_loop(0, acc_ref.shape[0], put, 0)


def cost(a, width):
    slots, rows, depth = a.shape
    return pl.CostEstimate(
        flops=2 * slots * rows * 256 * 768, bytes_accessed=8_000_000, transcendentals=0
    )


def first_stop(a, rows, homes, strips):
    width = strips.shape[-1]
    return pl.pallas_call(
        first_kernel,
        out_shape=jax.ShapeDtypeStruct((BRL, a.shape[1], width), jnp.float32),
        in_specs=[SMEM, SMEM, VMEM, VMEM],
        out_specs=VMEM,
        cost_estimate=cost(a, width),
        name="first_stop",
    )(rows, homes, a, strips)


def second_stop(a, rows, homes, place, strips, start, mask):
    width = strips.shape[-1]
    return pl.pallas_call(
        second_kernel,
        out_shape=jax.ShapeDtypeStruct((BRL, a.shape[1], width), jnp.bfloat16),
        in_specs=[SMEM, SMEM, SMEM, VMEM, VMEM, VMEM, VMEM],
        out_specs=VMEM,
        scratch_shapes=[pltpu.VMEM((BRL, a.shape[1], width), jnp.float32)],
        cost_estimate=cost(a, width),
        name="second_stop",
    )(rows, homes, place, a, strips, start, mask)


def unpack_kernel(src_ref, in_ref, out_ref):
    rest = out_ref.shape[-1] - LANES

    def step(l, carry):
        strip = in_ref[src_ref[l]]
        for j in range(BCL):
            out_ref[l, j, :, 0:LANES] = strip[:, j * LANES : (j + 1) * LANES]
            out_ref[l, j, :, LANES:] = strip[:, BCL * LANES + j * rest : BCL * LANES + (j + 1) * rest]
        return carry

    lax.fori_loop(0, out_ref.shape[0], step, 0)


def unpack(arrived, source, edge):
    return pl.pallas_call(
        unpack_kernel,
        out_shape=jax.ShapeDtypeStruct((BRL, BCL, arrived.shape[1], edge), jnp.bfloat16),
        in_specs=[SMEM, VMEM],
        out_specs=VMEM,
        name="unpack",
    )(source, arrived)


def homes_of(a_codes, b_codes):
    b_rows = b_codes // BCL
    slots = jnp.arange(b_codes.shape[0], dtype=jnp.int32)
    none = jnp.int32(b_codes.shape[0])

    def first_match(wanted):
        return jnp.min(jnp.where(wanted[:, None] == b_rows[None, :], slots[None, :], none), axis=1)

    return a_codes // KL, first_match(a_codes % KL), first_match(b_rows), b_codes % BCL


def body(a_blocks, a_coord, b_blocks, b_coord, keep_list, permutation):
    row_count = lax.axis_size("row")
    col_count = lax.axis_size("col")
    slot_count = BRL // row_count
    row_here = lax.axis_index("row")
    col_here = lax.axis_index("col")
    row_next = (row_here + 1) % row_count
    col_next = (col_here + 1) % col_count
    edge = a_blocks.shape[-1]
    parts = 3 if edge % 3 == 0 else 1
    size = edge // parts

    a_turned = a_blocks[0, 0].transpose(1, 2, 0)
    a_parts = [a_turned[q * size : (q + 1) * size] for q in range(parts)]

    b_first = b_blocks[0, 0, 0]
    b_sent = jnp.where(row_here == 0, b_blocks[0, 1, 0], b_first)
    sent_rest = b_sent[:, :, LANES:].transpose(1, 0, 2).reshape(edge, -1)
    moved_main = shifted(b_sent[:, :, :LANES], "row", -1)
    moved_rest = shifted(sent_rest, "row", -1)
    moved_rest = moved_rest.reshape(edge, b_first.shape[0], -1).transpose(1, 0, 2)
    a_moved = [shifted(part, "col", -1) for part in a_parts]

    rows1, homes1, b_homes1, b_cols1 = homes_of(
        a_coord[row_here, col_here], b_coord[row_here, 0, col_here]
    )
    image_pick = (row_next == 0).astype(jnp.int32)
    rows2, homes2, b_homes2, b_cols2 = homes_of(
        a_coord[row_here, col_next], b_coord[row_next, image_pick, col_here]
    )
    own_keep = keep_list[row_here, col_here]
    all_codes = jnp.arange(BRL * BCL, dtype=jnp.int32)
    keep_mask = jnp.any(all_codes[:, None] == own_keep[None, :], axis=1).reshape(BRL, BCL)
    keep_mask = keep_mask.astype(jnp.float32)
    rest = edge - LANES
    mask = jnp.concatenate(
        [
            jnp.repeat(keep_mask, LANES, axis=1),
            jnp.repeat(keep_mask, rest, axis=1),
            jnp.zeros((BRL, LANES - BCL * rest), jnp.float32),
        ],
        axis=1,
    )[:, None, :]

    targets = permutation.reshape(row_count, BRL)
    owners = targets // BRL
    positions = jnp.arange(BRL, dtype=jnp.int32)
    before = (owners[:, None, :] == owners[:, :, None]) & (
        positions[None, None, :] < positions[None, :, None]
    )
    slot_rank = jnp.sum(before.astype(jnp.int32), axis=2)
    place = owners[row_here] * slot_count + slot_rank[row_here]
    all_rows = jnp.arange(permutation.shape[0], dtype=jnp.int32)
    wanted = row_here * BRL + positions
    arrival = all_rows // BRL * slot_count + slot_rank.reshape(-1)
    source = jnp.sum(
        jnp.where(permutation[None, :] == wanted[:, None], arrival[None, :], 0), axis=1
    )

    strips1 = build_strips(b_first[:, :, :LANES], b_first[:, :, LANES:], b_homes1, b_cols1)
    starts = [first_stop(part.transpose(2, 0, 1), rows1, homes1, strips1) for part in a_parts]
    strips2 = build_strips(moved_main, moved_rest, b_homes2, b_cols2)
    done = []
    for q in range(parts):
        out = second_stop(
            a_moved[q].transpose(2, 0, 1), rows2, homes2, place, strips2, starts[q], mask
        )
        out = out.reshape((row_count, slot_count) + out.shape[1:])
        incoming = lax.all_to_all(out, "row", split_axis=0, concat_axis=0, tiled=True)
        done.append(unpack(incoming.reshape((BRL,) + incoming.shape[2:]), source, edge))
    return jnp.concatenate(done, axis=2)[None, None]


def solution(mesh):
    in_specs = (
        P("row", "col", None, None, None),
        P(),
        P("row", None, "col", None, None, None),
        P(),
        P(),
        P(),
    )
    out_specs = P("row", "col", None, None, None, None)
    return jax.shard_map(body, mesh=mesh, in_specs=in_specs, out_specs=out_specs, check_vma=False)
```

time: 610 us -> 312 us (0.51); the launches traced: 600 us -> 310 us
  local copies, waits for them, and re-layouts: 317 us -> 94.3 us
  matrix products: 167 us -> 0 us
  Pallas kernels: 0 us -> 166 us
  waiting for transfers between devices: 97.8 us -> 11.9 us
  other arithmetic: 5.57 us -> 15.7 us
  starting transfers between devices: 11.9 us -> 21.9 us
    dot_general x6 -> x0, matrix products: 167 us -> none  [the longest x2 75.4 us: panel_product(): jnp.einsum('si,sjac->ijac', placing, terms, precision=lax.Precision.HIGHEST)]
    pallas_call x0 -> x11, Pallas kernels: none -> 166 us  [the longest x3 71.6 us: second_stop(): pl.pallas_call(second_kernel, out_shape=jax.ShapeDtypeStruct((BRL, a.shap...]
    convert_element_type x3 -> x1, local copies, waits for them, and re-layouts: 121 us -> 0.08 us  [body(): keep_mask = keep_mask.astype(jnp.float32)]
    transpose x2 -> x3, local copies, waits for them, and re-layouts: 121 us -> 11.2 us  [the longest x1 8.23 us: body(): part.transpose(2, 0, 1)]
    all_to_all x1 -> x3, waiting for transfers between devices: 97.8 us -> 11.9 us  [body(): lax.all_to_all(out, 'row', split_axis=0, concat_axis=0, tiled=True)]
    scatter x2 -> x0, local copies, waits for them, and re-layouts: 19.1 us -> none  [the longest x1 18.4 us: body(): outgoing.at[owners[row_here], slot_rank[row_here]]]
    slice x1 -> x7, local copies, waits for them, and re-layouts: 13.2 us -> 31.7 us  [the longest x3 14 us: body(): a_parts = [a_turned[q * size:(q + 1) * size] for q in range(parts)]]
    unnamed x10 -> x14, local copies, waits for them, and re-layouts: 0.02 us -> 13.7 us
  transfers between devices with their start and end apart: 3 -> 8, of which waited for: 1 -> 1; matrix products, arithmetic and copies ran while one was open for 48% -> 24% of each run, Pallas kernels for 0% -> 52%
where the time goes in v1:
time: 312 us; the launch traced here: 310 us
  Pallas kernels  166 us (53%)
  local copies, waits for them, and re-layouts  94.3 us (30%)
  starting transfers between devices  21.9 us (7%)
  other arithmetic  15.7 us (5%)
  waiting for transfers between devices  11.9 us (4%)
    pallas_call x3, Pallas kernels, second_stop(): pl.pallas_call(second_kernel, out_shape=jax.ShapeDtypeStruct((BRL, a.shap...  71.6 us
    pallas_call x3, Pallas kernels, first_stop(): pl.pallas_call(first_kernel, out_shape=jax.ShapeDtypeStruct((BRL, a.shape...  70.1 us
    ppermute x3, local copies, waits for them, and re-layouts, shifted(): return lax.ppermute(value, axis, pairs)  17.1 us
    all_to_all x3, starting transfers between devices, body(): lax.all_to_all(out, 'row', split_axis=0, concat_axis=0, tiled=True)  14.1 us
    slice x3, local copies, waits for them, and re-layouts, body(): a_parts = [a_turned[q * size:(q + 1) * size] for q in range(parts)]  14 us
    unnamed x14, local copies, waits for them, and re-layouts  13.7 us
    slice x1, local copies, waits for them, and re-layouts, body(): b_first = b_blocks[0, 0, 0]  13.1 us
    pallas_call x2, Pallas kernels, build_strips(): pl.pallas_call(strip_kernel, out_shape=jax.ShapeDtypeStruct((slots + 1, e...  13.1 us
  transfers between devices with their start and end apart: 8, of which 1 were waited for; matrix products, arithmetic and copies ran while one was open for 24% of the time, Pallas kernels for 52%

profile of v1, /device:TPU:0, one launch (start us, length us, event | category | flops | bytes accessed | tf_op | source)
XLA Modules:
  0.0 310.2 jit_solution(7582512788809410000)
XLA Ops:
  0.0 13.6 %copy.35 = bf16[1,1,108,138,138]{4,3,2,1,0:T(8,128)(2,1)} copy(bf16[1,1,108,138,138]{2,4,3,1,0:T(8,128)(2,1)} %param.6) | data formatting | bytes 8227008 | tf_op args[0]
  13.6 8.2 %slice_bitcast_fusion.3 = (bf16[108,46,138]{2,1,0:T(8,128)(2,1)}, bf16[108,46,138]{2,1,0:T(8,128)(2,1)}, bf16[108,46,138]{2,1,0:T(8,128)(2,1)}, bf16[46,138,108]...) fusion(bf16[138,138,108]{1,0,2:T(8,128)(2,1)} %bitcast.70), kind=kLoop, calls=%fused_computation.61 | loop fusion | bytes 12340512 | tf_op jit(solution)/shard_map/transpose | solution.py:207
  21.9 5.2 %copy.48 = bf16[46,138,108]{2,1,0:T(8,128)(2,1)} copy(bf16[46,138,108]{1,0,2:T(8,128)(2,1)} %get-tuple-element.14) | data formatting | bytes 2742336 | tf_op jit(solution)/shard_map/slice | solution.py:160
  27.0 3.4 %collective-permute-start.4 = (bf16[46,138,108]{2,1,0:T(8,128)(2,1)}, bf16[46,138,108]{2,1,0:T(8,128)(2,1)}, u32[]{:S(2)}, u32[]{:S(2)}) collective-permute-start(bf16[46,138,108]{2,1,0:T(8,128)(2,1)} %copy.48), channel_id=1, source_target_pairs={{0,7},{1,0},{2,1},{3,2},{4,3},{5,4},{6,5},{7,6},{8,15},{9,8},{10,9... | collective-permute-start | bytes 4113512 | tf_op jit(solution)/shard_map/ppermute | solution.py:19
  30.4 13.1 %fusion.15 = (bf16[1,1,1,27,138,138]{5,1,4,3,2,0:T(2,128)(2,1)}, bf16[1,1,1,27,138,138]{5,1,4,3,2,0:T(2,128)(2,1)}) fusion(bf16[1,2,1,27,138,138]{5,1,4,3,2,0:T(2,128)(2,1)} %param.8), kind=kLoop, calls=%fused_computation.62 | loop fusion | bytes 4113504 | tf_op jit(solution)/shard_map/slice | solution.py:162
  43.5 5.0 %fusion = (bf16[27,138,138]{2,1,0:T(8,128)(2,1)S(1)}, bf16[27,138,138]{2,1,0:T(8,128)(2,1)}) fusion(bf16[1,1,1,27,138,138]{5,1,4,3,2,0:T(2,128)(2,1)} %get-tuple-element.18, pred[]{:T(512)S(6)} %eq.121, bf16[1,1,1,27,138,138]{5,1,4,3,2,0:T(2,128)(2,1)} %get-tuple-element.17), kind=kLoop, calls=%fused_computation.3 | loop fusion | flops 514188 | bytes 4113505 | tf_op jit(solution)/shard_map/jit(_where)/select_n | solution.py:163
  48.5 1.1 slice.37
  49.6 3.6 %collective-permute-start.1 = (bf16[27,138,128]{2,1,0:T(8,128)(2,1)}, bf16[27,138,128]{2,1,0:T(8,128)(2,1)}, u32[]{:S(2)}, u32[]{:S(2)}) collective-permute-start(bf16[27,138,128]{2,1,0:T(8,128)(2,1)} %slice.37), channel_id=1, source_target_pairs={{0,24},{8,0},{16,8},{24,16},{1,25},{9,1},{17,9},{25,17},{2,26},{10... | collective-permute-start | bytes 2861576 | tf_op jit(solution)/shard_map/ppermute | solution.py:19
  53.2 1.2 slice_bitcast_fusion
  54.4 1.8 copy.40
  56.2 0.1 reshape.286
  56.3 0.5 collective-permute-start.2
  56.8 5.2 %copy.44 = bf16[46,138,108]{2,1,0:T(8,128)(2,1)} copy(bf16[46,138,108]{1,0,2:T(8,128)(2,1)} %get-tuple-element.15) | data formatting | bytes 2742336 | tf_op jit(solution)/shard_map/slice | solution.py:160
  62.0 0.1 collective-permute-start.3
  62.1 2.4 slice.39.main_ref
  64.5 1.1 slice.40.rest_ref
  65.6 0.1 reshape.284
  65.7 1.2 and_select_fusion
  66.9 0.1 fusion.1
  67.0 0.1 reshape.296
  67.1 0.1 broadcast_in_dim.92
  67.2 0.1 reshape.289
  67.2 0.1 broadcast_in_dim.91
  67.3 0.1 pad.5.clone
  67.4 0.6 broadcast_in_dim.94.mask_ref
  68.1 1.3 and_select_fusion.3
  69.4 0.8 select_reduce_fusion.home_ref
  70.1 6.5 %strips.3.strip_ref = bf16[28,138,640]{2,1,0:T(8,128)(2,1)} custom-call(s32[27]{0:T(128)} %select_reduce_fusion.home_ref, s32[27]{0:T(128)} %get-tuple-element.5.col_ref, bf16[27,138,128]{2,1,0:T(8,128)(2,1)} %slice.39.main_ref, bf16[27,138,10]{2,1,0:T(8,128)(2,1)} %slice.40.rest_ref), custom_call_target="tpu_custom_call" | custom-call | tf_op jit(solution)/shard_map/strips/pallas_call | solution.py:43
  76.6 1.4 and_select_fusion.2
  78.0 0.7 select_reduce_fusion.2.home_ref
  78.7 0.2 convert_reduce_fusion
  78.9 0.7 select_reduce_fusion.1
  79.6 23.4 %first_stop.5.start_ref = f32[16,46,640]{2,1,0:T(8,128)} custom-call(s32[108]{0:T(128)} %get-tuple-element.22.row_ref, s32[108]{0:T(128)} %get-tuple-element.24.home_ref, bf16[108,46,138]{2,1,0:T(8,128)(2,1)} %get-tuple-element.13.a_ref, bf16[28,138,640]{2,1,0:T(8,128)(2,1)} %strips.3.strip_ref), custom_call_target="tpu_custom_call" | custom-call | flops 1953497088 | bytes 8000000 | tf_op jit(solution)/shard_map/first_stop/pallas_call | solution.py:90
  103.0 0.5 fusion.13.place_ref
  103.5 0.1 reshape.287
  103.6 1.5 copy.41
  105.1 6.6 %strips.2.strip_ref = bf16[28,138,640]{2,1,0:T(8,128)(2,1)} custom-call(s32[27]{0:T(128)} %select_reduce_fusion.2.home_ref, s32[27]{0:T(128)} %get-tuple-element.9.col_ref, bf16[27,138,128]{2,1,0:T(8,128)(2,1)} %collective-permute-done.1.main_ref, bf16[27,138,10]{2,1,0:T(8,128)(2,1)} %bitcast.74), custom_call_target="tpu_custom_call" | custom-call | tf_op jit(solution)/shard_map/strips/pallas_call | solution.py:43
  111.7 5.8 %copy.49 = bf16[46,138,108]{1,0,2:T(8,128)(2,1)} copy(bf16[46,138,108]{2,1,0:T(8,128)(2,1)} %collective-permute-done.4) | data formatting | bytes 2742336 | tf_op jit(solution)/shard_map/ppermute | solution.py:19
  117.5 23.8 %second_stop.5 = bf16[16,46,640]{2,1,0:T(8,128)(2,1)} custom-call(s32[108]{0:T(128)} %get-tuple-element.23.row_ref, s32[108]{0:T(128)} %get-tuple-element.25.home_ref, s32[16]{0:T(128)} %fusion.13.place_ref, bf16[108,46,138]{2,1,0:T(8,128)(2,1)} %bitcast.72, bf16[28,138,640]{2,1,0:T(8,128)(2,1)} %strips.2.strip_ref, f32[16,46,640]{2,1,0:T(8,128)} %first_stop.5.start_ref, ...), custom_call_target="tpu_custom_call" | custom-call | flops 1953497088 | bytes 8000000 | tf_op jit(solution)/shard_map/second_stop/pallas_call | solution.py:102
  141.3 2.5 copy.50
  143.9 4.2 %all-to-all-start.2 = ((bf16[4,4,46,640]{3,1,2,0:T(4,128)(2,1)}), bf16[4,4,46,640]{3,1,2,0:T(4,128)(2,1)}, u32[]{:S(2)}, u32[]{:S(2)}) async-start(bf16[4,4,46,640]{3,1,2,0:T(4,128)(2,1)} %copy.50), calls=%async_computation.2 | async-start | bytes 1884160 | tf_op jit(solution)/shard_map/all_to_all | solution.py:215
  148.1 3.7 %copy.36 = bf16[46,138,108]{2,1,0:T(8,128)(2,1)} copy(bf16[46,138,108]{1,0,2:T(8,128)(2,1)S(1)} %get-tuple-element.16) | data formatting | bytes 2742336 | tf_op jit(solution)/shard_map/slice | solution.py:160
  151.8 0.2 collective-permute-start
  152.0 23.4 %first_stop.4.start_ref = f32[16,46,640]{2,1,0:T(8,128)} custom-call(s32[108]{0:T(128)} %get-tuple-element.22.row_ref, s32[108]{0:T(128)} %get-tuple-element.24.home_ref, bf16[108,46,138]{2,1,0:T(8,128)(2,1)} %get-tuple-element.12.a_ref, bf16[28,138,640]{2,1,0:T(8,128)(2,1)} %strips.3.strip_ref), custom_call_target="tpu_custom_call" | custom-call | flops 1953497088 | bytes 8000000 | tf_op jit(solution)/shard_map/first_stop/pallas_call | solution.py:90
  175.4 5.8 %copy.45 = bf16[46,138,108]{1,0,2:T(8,128)(2,1)} copy(bf16[46,138,108]{2,1,0:T(8,128)(2,1)} %collective-permute-done.3) | data formatting | bytes 2742336 | tf_op jit(solution)/shard_map/ppermute | solution.py:19
  181.2 23.9 %second_stop.4 = bf16[16,46,640]{2,1,0:T(8,128)(2,1)} custom-call(s32[108]{0:T(128)} %get-tuple-element.23.row_ref, s32[108]{0:T(128)} %get-tuple-element.25.home_ref, s32[16]{0:T(128)} %fusion.13.place_ref, bf16[108,46,138]{2,1,0:T(8,128)(2,1)} %bitcast.73, bf16[28,138,640]{2,1,0:T(8,128)(2,1)} %strips.2.strip_ref, f32[16,46,640]{2,1,0:T(8,128)} %first_stop.4.start_ref, ...), custom_call_target="tpu_custom_call" | custom-call | flops 1953497088 | bytes 8000000 | tf_op jit(solution)/shard_map/second_stop/pallas_call | solution.py:102
  205.0 2.5 copy.46
  207.6 4.8 %all-to-all-start.1 = ((bf16[4,4,46,640]{3,1,2,0:T(4,128)(2,1)}), bf16[4,4,46,640]{3,1,2,0:T(4,128)(2,1)S(1)}, u32[]{:S(2)}, u32[]{:S(2)}) async-start(bf16[4,4,46,640]{3,1,2,0:T(4,128)(2,1)} %copy.46), calls=%async_computation.1 | async-start | bytes 1884160 | tf_op jit(solution)/shard_map/all_to_all | solution.py:215
  212.4 23.3 %first_stop.3.start_ref = f32[16,46,640]{2,1,0:T(8,128)} custom-call(s32[108]{0:T(128)} %get-tuple-element.22.row_ref, s32[108]{0:T(128)} %get-tuple-element.24.home_ref, bf16[108,46,138]{2,1,0:T(8,128)(2,1)} %get-tuple-element.11.a_ref, bf16[28,138,640]{2,1,0:T(8,128)(2,1)} %strips.3.strip_ref), custom_call_target="tpu_custom_call" | custom-call | flops 1953497088 | bytes 8000000 | tf_op jit(solution)/shard_map/first_stop/pallas_call | solution.py:90
  235.7 5.6 %copy.37 = bf16[46,138,108]{1,0,2:T(8,128)(2,1)} copy(bf16[46,138,108]{2,1,0:T(8,128)(2,1)S(1)} %collective-permute-done) | data formatting | bytes 2742336 | tf_op jit(solution)/shard_map/ppermute | solution.py:19
  241.3 23.9 %second_stop.3 = bf16[16,46,640]{2,1,0:T(8,128)(2,1)} custom-call(s32[108]{0:T(128)} %get-tuple-element.23.row_ref, s32[108]{0:T(128)} %get-tuple-element.25.home_ref, s32[16]{0:T(128)} %fusion.13.place_ref, bf16[108,46,138]{2,1,0:T(8,128)(2,1)} %bitcast.71, bf16[28,138,640]{2,1,0:T(8,128)(2,1)} %strips.2.strip_ref, f32[16,46,640]{2,1,0:T(8,128)} %first_stop.3.start_ref, ...), custom_call_target="tpu_custom_call" | custom-call | flops 1953497088 | bytes 8000000 | tf_op jit(solution)/shard_map/second_stop/pallas_call | solution.py:102
  265.2 2.5 copy.42
  267.7 5.1 %all-to-all-start = ((bf16[4,4,46,640]{3,1,2,0:T(4,128)(2,1)}), bf16[4,4,46,640]{3,1,2,0:T(4,128)(2,1)}, u32[]{:S(2)}, u32[]{:S(2)}) async-start(bf16[4,4,46,640]{3,1,2,0:T(4,128)(2,1)} %copy.42), calls=%async_computation | async-start | bytes 1884160 | tf_op jit(solution)/shard_map/all_to_all | solution.py:215
  272.8 0.1 reshape.285
  272.9 0.7 select_reduce_fusion.4.src_ref
  273.6 2.3 copy.51
  275.8 3.8 %unpack.5 = bf16[16,4,46,138]{3,2,1,0:T(8,128)(2,1)} custom-call(s32[16]{0:T(128)} %select_reduce_fusion.4.src_ref, bf16[16,46,640]{2,1,0:T(8,128)(2,1)} %bitcast.79), custom_call_target="tpu_custom_call" | custom-call | tf_op jit(solution)/shard_map/unpack/pallas_call | solution.py:127
  279.6 1.1 copy.47
  280.7 3.8 %unpack.4 = bf16[16,4,46,138]{3,2,1,0:T(8,128)(2,1)} custom-call(s32[16]{0:T(128)} %select_reduce_fusion.4.src_ref, bf16[16,46,640]{2,1,0:T(8,128)(2,1)} %bitcast.80), custom_call_target="tpu_custom_call" | custom-call | tf_op jit(solution)/shard_map/unpack/pallas_call | solution.py:127
  284.6 11.9 %all-to-all-done = bf16[4,4,46,640]{3,1,2,0:T(4,128)(2,1)} async-done(((bf16[4,4,46,640]{3,1,2,0:T(4,128)(2,1)}), bf16[4,4,46,640]{3,1,2,0:T(4,128)(2,1)}, u32[]{:S(2)}, u32[]{:S(2)}) %all-to-all-start) | async-done | bytes 942112 | tf_op jit(solution)/shard_map/all_to_all | solution.py:215
  296.4 2.3 copy.43
  298.7 3.8 %unpack.3 = bf16[16,4,46,138]{3,2,1,0:T(8,128)(2,1)} custom-call(s32[16]{0:T(128)} %select_reduce_fusion.4.src_ref, bf16[16,46,640]{2,1,0:T(8,128)(2,1)} %bitcast.78), custom_call_target="tpu_custom_call" | custom-call | tf_op jit(solution)/shard_map/unpack/pallas_call | solution.py:127
  302.6 3.2 %maximum_bitcast_fusion = bf16[1,1,16,4,138,138]{5,4,3,2,1,0:T(8,128)(2,1)S(1)} fusion(bf16[16,4,46,138]{3,2,1,0:T(8,128)(2,1)S(1)} %copy-done.3, bf16[16,4,46,138]{3,2,1,0:T(8,128)(2,1)S(1)} %copy-done.4, bf16[16,4,46,138]{3,2,1,0:T(8,128)(2,1)} %unpack.3), kind=kLoop, calls=%fused_computation | loop fusion | flops 7312896 | bytes 4875264 | tf_op jit(solution)/shard_map/broadcast_in_dim | solution.py:217
  305.7 4.4 %copy.52 = bf16[1,1,16,4,138,138]{5,3,4,2,1,0:T(4,128)(2,1)} copy(bf16[1,1,16,4,138,138]{5,4,3,2,1,0:T(8,128)(2,1)S(1)} %maximum_bitcast_fusion) | data formatting | bytes 4875264 | tf_op jit(solution)/shard_map/broadcast_in_dim | solution.py:217
  (29 shorter events, 0.1 us)
Async XLA Ops:
  0.0 66.9 %copy-start = (s32[4,8,32]{2,1,0:T(8,128)S(1)}, s32[4,8,32]{2,1,0:T(8,128)}, u32[]{:S(2)}) copy-start(s32[4,8,32]{2,1,0:T(8,128)} %param.10) | copy-start | bytes 12292
  27.0 84.7 %collective-permute-start.4 = (bf16[46,138,108]{2,1,0:T(8,128)(2,1)}, bf16[46,138,108]{2,1,0:T(8,128)(2,1)}, u32[]{:S(2)}, u32[]{:S(2)}) collective-permute-start(bf16[46,138,108]{2,1,0:T(8,128)(2,1)} %copy.48), channel_id=1, source_target_pairs={{0,7},{1,0},{2,1},{3,2},{4,3},{5,4},{6,5},{7,6},{8,15},{9,8},{10,9... | collective-permute-start | bytes 4113512 | tf_op jit(solution)/shard_map/ppermute | solution.py:19
  49.6 55.5 %collective-permute-start.1 = (bf16[27,138,128]{2,1,0:T(8,128)(2,1)}, bf16[27,138,128]{2,1,0:T(8,128)(2,1)}, u32[]{:S(2)}, u32[]{:S(2)}) collective-permute-start(bf16[27,138,128]{2,1,0:T(8,128)(2,1)} %slice.37), channel_id=1, source_target_pairs={{0,24},{8,0},{16,8},{24,16},{1,25},{9,1},{17,9},{25,17},{2,26},{10... | collective-permute-start | bytes 2861576 | tf_op jit(solution)/shard_map/ppermute | solution.py:19
  56.3 47.2 %collective-permute-start.2 = (bf16[138,270]{0,1:T(8,128)(2,1)S(1)}, bf16[138,270]{0,1:T(8,128)(2,1)S(1)}, u32[]{:S(2)}, u32[]{:S(2)}) collective-permute-start(bf16[138,270]{0,1:T(8,128)(2,1)S(1)} %reshape.286), channel_id=1, source_target_pairs={{0,24},{8,0},{16,8},{24,16},{1,25},{9,1},{17,9},{25,17},{2,26},{10... | collective-permute-start | bytes 223568 | tf_op jit(solution)/shard_map/ppermute | solution.py:19
  62.0 3.6 %copy-start.5 = (s32[64]{0:T(128)S(1)}, s32[64]{0:T(128)}, u32[]{:S(2)}) copy-start(s32[64]{0:T(128)} %param.11) | copy-start | bytes 772
  62.0 113.4 %collective-permute-start.3 = (bf16[46,138,108]{2,1,0:T(8,128)(2,1)}, bf16[46,138,108]{2,1,0:T(8,128)(2,1)}, u32[]{:S(2)}, u32[]{:S(2)}) collective-permute-start(bf16[46,138,108]{2,1,0:T(8,128)(2,1)} %copy.44), channel_id=1, source_target_pairs={{0,7},{1,0},{2,1},{3,2},{4,3},{5,4},{6,5},{7,6},{8,15},{9,8},{10,9... | collective-permute-start | bytes 4113512 | tf_op jit(solution)/shard_map/ppermute | solution.py:19
  62.1 2.4 copy-start.2
  143.9 63.7 %all-to-all-start.2 = ((bf16[4,4,46,640]{3,1,2,0:T(4,128)(2,1)}), bf16[4,4,46,640]{3,1,2,0:T(4,128)(2,1)}, u32[]{:S(2)}, u32[]{:S(2)}) async-start(bf16[4,4,46,640]{3,1,2,0:T(4,128)(2,1)} %copy.50), calls=%async_computation.2 | async-start | bytes 1884160 | tf_op jit(solution)/shard_map/all_to_all | solution.py:215
  151.8 84.0 %collective-permute-start = (bf16[46,138,108]{2,1,0:T(8,128)(2,1)}, bf16[46,138,108]{2,1,0:T(8,128)(2,1)S(1)}, u32[]{:S(2)}, u32[]{:S(2)}) collective-permute-start(bf16[46,138,108]{2,1,0:T(8,128)(2,1)} %copy.36), channel_id=1, source_target_pairs={{0,7},{1,0},{2,1},{3,2},{4,3},{5,4},{6,5},{7,6},{8,15},{9,8},{10,9... | collective-permute-start | bytes 4113512 | tf_op jit(solution)/shard_map/ppermute | solution.py:19
  207.6 60.1 %all-to-all-start.1 = ((bf16[4,4,46,640]{3,1,2,0:T(4,128)(2,1)}), bf16[4,4,46,640]{3,1,2,0:T(4,128)(2,1)S(1)}, u32[]{:S(2)}, u32[]{:S(2)}) async-start(bf16[4,4,46,640]{3,1,2,0:T(4,128)(2,1)} %copy.46), calls=%async_computation.1 | async-start | bytes 1884160 | tf_op jit(solution)/shard_map/all_to_all | solution.py:215
  267.7 28.8 %all-to-all-start = ((bf16[4,4,46,640]{3,1,2,0:T(4,128)(2,1)}), bf16[4,4,46,640]{3,1,2,0:T(4,128)(2,1)}, u32[]{:S(2)}, u32[]{:S(2)}) async-start(bf16[4,4,46,640]{3,1,2,0:T(4,128)(2,1)} %copy.42), calls=%async_computation | async-start | bytes 1884160 | tf_op jit(solution)/shard_map/all_to_all | solution.py:215
  284.5 18.0 %copy-start.3 = (bf16[16,4,46,138]{3,2,1,0:T(8,128)(2,1)S(1)}, bf16[16,4,46,138]{3,2,1,0:T(8,128)(2,1)}, u32[]{:S(2)}) copy-start(bf16[16,4,46,138]{3,2,1,0:T(8,128)(2,1)} %unpack.5) | copy-start | bytes 2437636
  284.5 18.0 %copy-start.4 = (bf16[16,4,46,138]{3,2,1,0:T(8,128)(2,1)S(1)}, bf16[16,4,46,138]{3,2,1,0:T(8,128)(2,1)}, u32[]{:S(2)}) copy-start(bf16[16,4,46,138]{3,2,1,0:T(8,128)(2,1)} %unpack.4) | copy-start | bytes 2437636
  302.6 7.6 %copy-start.1 = (s32[4,8,32]{2,1,0:T(8,128)S(1)}, s32[4,8,32]{2,1,0:T(8,128)}, u32[]{:S(2)}) copy-start(s32[4,8,32]{2,1,0:T(8,128)} %param.10) | copy-start | bytes 12292
